TPU v7x, 512 devices: a whole 4x8x8 slice. The times are simulated.
512 devices in a mesh: iface: 512 (over y, z, x, core).
Axes of the slice: x: 4, y: 8, z: 8, core: 2. Of those that a mesh axis runs over, the one named last changes fastest.
Arguments:
- res_diffs: float32 [128, 2, 1048576], P(None, None, 'iface'), may hold values from -400 to 400, as said below
- out_diffs: float32 [128, 2, 1048576], P(None, None, 'iface'), may hold values from -0.5 to 0.5
- residual: float32 [2, 1048576], P(None, 'iface'), may hold values from -60000 to 60000
Outputs:
- correction: float32 [2, 1048576], P(None, 'iface')
- coefficients: float32 [128], replicated
Inputs may be any that keep to these rules, and one draw needn't show every extreme that they name: `res_diffs`: columns are linearly independent.
All inputs are finite; a program needn't handle non-finite values.
Results may differ from a plain program's by a relative error of at most 0.00016.
Values sent between devices are 32-bit elements; how exact they have to be, the bound alone decides.
No kernel may reach another device: no remote copies, remote signals or barrier semaphores. Data moves between devices by JAX's collectives and lax.ppermute only.
A program may use at most 64 MiB of HBM per device.

v0:
```python
import jax
import jax.numpy as jnp
from jax import lax
from jax.sharding import PartitionSpec as P


def solve_factored(lower, vector):
    column = vector[:, None]
    middle = lax.linalg.triangular_solve(lower, column, left_side=True, lower=True)
    result = lax.linalg.triangular_solve(
        lower, middle, left_side=True, lower=True, transpose_a=True
    )
    return result[:, 0]


def on_device(res_diffs, out_diffs, residual):
    precise = lax.Precision.HIGHEST
    rows_all = residual.shape[1] * lax.axis_size("iface")
    squares = jnp.sum(residual * residual, axis=1)
    total = lax.psum(squares, "iface")
    weights = lax.rsqrt(total / rows_all + 1e-06)
    scaled = res_diffs * weights[None, :, None]
    target = residual * weights[:, None]
    local_gram = jnp.einsum("mfi,nfi->mn", scaled, scaled, precision=precise)
    local_proj = jnp.einsum("mfi,fi->m", scaled, target, precision=precise)
    gram, proj = lax.psum((local_gram, local_proj), "iface")
    lower_part = jnp.linalg.cholesky(gram)
    coefficients = -solve_factored(lower_part, proj)
    correction = jnp.einsum("mfi,m->fi", out_diffs, coefficients, precision=precise)
    return (correction, coefficients)


def solution(mesh):
    placed = (P(None, None, "iface"), P(None, None, "iface"), P(None, "iface"))
    return jax.shard_map(
        on_device, mesh=mesh, in_specs=placed, out_specs=(P(None, "iface"), P()), check_vma=False
    )
```

profile of v0, /device:TPU:1, one launch (start us, length us, event | category | flops | bytes accessed | tf_op | source)
XLA Modules:
  0.0 415.3 jit_solution(10357398860026261465)
XLA Ops:
  7.2 0.0 copy-start
  7.2 0.0 all-reduce.2.cloned.1.call-start
  7.2 1.0 multiply_reduce_fusion
  8.2 106.1 %psum.21 = f32[2]{0:T(128)S(1)} all-reduce(f32[2]{0:T(128)S(1)} %multiply_reduce_fusion), channel_id=1, replica_groups=mesh['iface'=512] {'iface'}, use_global_device_ids=true, to_apply=%region_1.0 | all-reduce | flops 2 | bytes 16 | tf_op jit(solution)/shard_map/psum | solution.py:20
  114.3 2.7 broadcast_multiply_fusion
  117.0 0.0 copy-start.1
  117.1 1.3 copy-done.1
  118.4 0.0 copy-start.2
  118.4 4.7 %fusion.6 = f32[128,128]{0,1:T(8,128)} fusion(f32[128,2,2048]{2,1,0:T(2,128)S(1)} %broadcast_multiply_fusion), kind=kOutput, calls=%fused_computation.6 | convolution fusion | flops 805306368 | bytes 2162688 | tf_op jit(solution)/shard_map/mfi,nfi->mn/dot_general | solution.py:24
  123.1 0.0 all-reduce.2.cloned.1.call-update
  123.1 0.0 copy-done.2
  123.1 0.1 multiply_bitcast_fusion
  123.2 4.2 %fusion.10 = f32[128]{0:T(128)S(1)} fusion(f32[128,2,2048]{2,1,0:T(2,128)} %copy-done.1, f32[2,2048,1]{1,0,2:T(2,128)S(1)} %multiply_bitcast_fusion), kind=kOutput, calls=%fused_computation.10 | convolution fusion | flops 6291456 | bytes 2114048 | tf_op jit(solution)/shard_map/mfi,fi->m/dot_general | solution.py:25
  127.4 95.1 %psum.23 = f32[128]{0:T(128)S(1)} all-reduce(f32[128]{0:T(128)S(1)} %fusion.10), channel_id=1, replica_groups=mesh['iface'=512] {'iface'}, use_global_device_ids=true, to_apply=%region_5.6 | all-reduce | flops 128 | bytes 1024 | tf_op jit(solution)/shard_map/psum | solution.py:26
  222.5 158.1 %all-reduce.2.cloned.1.call-done = f32[128,128]{0,1:T(8,128)} async-done(((f32[128,128]{0,1:T(8,128)}), f32[128,128]{0,1:T(8,128)}) %all-reduce.2.cloned.1.call-update) | async-done | bytes 65552 | tf_op jit(solution)/shard_map/psum | solution.py:26
  380.6 0.9 copy.8
  381.5 0.9 fusion.16
  382.4 11.7 %cholesky.16 = f32[128,128]{1,0:T(8,128)S(1)} custom-call(f32[128,128]{1,0:T(8,128)S(1)} %fusion.16), custom_call_target="Cholesky" | custom-call | tf_op jit(solution)/shard_map/jit(cholesky)/cholesky | solution.py:27
  394.1 0.6 compare_reduce_fusion
  394.8 0.7 fusion.13
  395.4 9.8 %custom-call.8 = f32[1,128,128]{1,2,0:T(8,128)S(1)} custom-call(f32[1,128,128]{2,1,0:T(8,128)S(1)} %fusion.13), custom_call_target="InvertDiagBlocksLowerTriangular" | custom-call | tf_op jit(solution)/shard_map/triangular_solve | solution.py:10
  405.2 0.2 convolution_bitcast_fusion.1
  405.4 0.2 fusion.9
  405.6 0.0 copy-done
  405.6 0.0 copy-start.3
  405.6 2.2 fusion
  407.9 0.6 copy.27
  408.5 0.0 copy-done.3
  (2 shorter events, 0.0 us)
Async XLA Ops:
  7.2 398.4 %copy-start = (f32[128,2,2048]{2,1,0:T(2,128)S(1)}, f32[128,2,2048]{2,1,0:T(2,128)}, u32[]{:S(2)}) copy-start(f32[128,2,2048]{2,1,0:T(2,128)} %param.4) | copy-start | bytes 6291460
  7.2 373.4 %all-reduce.2.cloned.1.call-start = ((), (), s32[]{:S(2)}) async-start(), calls=%async_computation | async-start | bytes 131072 | tf_op jit(solution)/shard_map/psum | solution.py:26
  117.0 1.4 copy-start.1
  118.4 4.7 %copy-start.2 = (f32[2,2048]{1,0:T(2,128)S(1)}, f32[2,2048]{1,0:T(2,128)}, u32[]{:S(2)}) copy-start(f32[2,2048]{1,0:T(2,128)} %param.5) | copy-start | bytes 49156
  405.6 2.9 copy-start.3
Sparse Core Ops, SparseCore 0:
  123.2 257.3 all-reduce.1
where the time goes:
time: 416 us; the launch traced here: 415 us
  blocking collectives  201 us (48%)
  waiting for transfers between devices  158 us (38%)
  other arithmetic  27.5 us (7%)
  between operations  14.1 us (3%)
  matrix products  11.5 us (3%)
    psum x1, waiting for transfers between devices, on_device(): gram, proj = lax.psum((local_gram, local_proj), 'iface')  158 us
    psum x1, blocking collectives, on_device(): total = lax.psum(squares, 'iface')  106 us
    psum x1, blocking collectives, on_device(): gram, proj = lax.psum((local_gram, local_proj), 'iface')  95.1 us
    another operation x3, other arithmetic, on_device(): lower_part = jnp.linalg.cholesky(gram)  12.4 us
    another operation x2, other arithmetic, solve_factored(): lax.linalg.triangular_solve(lower, middle, left_side=True, lower=True, tr...  10.5 us
  transfers between devices with their start and end apart: 1, of which 1 were waited for; matrix products, arithmetic and copies ran while one was open for 1% of the time, Pallas kernels for 0%

commit v1 on v0

v1 whole, which is shorter than its diff:
```python
import jax
import jax.numpy as jnp
from jax import lax
from jax.experimental import pallas as pl
from jax.experimental.pallas import tpu as pltpu
from jax.sharding import PartitionSpec as P

AXIS = "iface"
LANES = 128
EPSILON = 1e-06
TOLERANCE = 1e-06
STEPS_MAX = 16
INNER = ("y0", "x1", "x0", "c")
BITS = ("y2", "y1", "y0", "z2", "z1", "z0", "x1", "x0", "c")


def groups_over(names):
    count = len(BITS)
    found = {}
    for device in range(1 << count):
        bits = [(device >> (count - 1 - k)) & 1 for k in range(count)]
        key = tuple(b for b, name in zip(bits, BITS) if name not in names)
        found.setdefault(key, []).append(device)
    return list(found.values())


def rows_of(x):
    lead = x.shape[:-2]
    fields, n = x.shape[-2:]
    blocks = x.reshape(lead + (fields, n // LANES, LANES))
    return jnp.swapaxes(blocks, -3, -2).reshape(lead + (fields * n // LANES, LANES))


def eye_mask(m):
    return lax.broadcasted_iota(jnp.int32, (m, m), 0) == lax.broadcasted_iota(jnp.int32, (m, m), 1)


def as_row(column, eye):
    return jnp.sum(jnp.where(eye, column, 0.0), axis=0, keepdims=True)


def as_column(row, eye):
    m = eye.shape[0]
    return jnp.broadcast_to(jnp.sum(jnp.where(eye, row, 0.0), axis=1, keepdims=True), (m, m))


def gram_kernel(diffs_ref, residual_ref, out_ref, staged, parts, sems):
    m = diffs_ref.shape[0]
    rows = diffs_ref.shape[1]
    order = [*range(0, rows, 2), *range(1, rows, 2)]
    copies = {}
    for j in order:
        copies[j] = pltpu.make_async_copy(diffs_ref.at[:, j, :], staged.at[j], sems.at[j])
        copies[j].start()
    eye = eye_mask(m)
    residual = residual_ref[...]
    parity = lax.broadcasted_iota(jnp.int32, residual.shape, 0) & 1
    grams, projs, squares = [], [], []
    for f in range(2):
        proj = None
        for k in range(rows // 2):
            j = 2 * k + f
            copies[j].wait()
            block = staged[j]
            term = block * residual_ref[j : j + 1, :]
            proj = term if proj is None else proj + term
            high = block.astype(jnp.bfloat16)
            rest = block - high.astype(jnp.float32)
            middle = rest.astype(jnp.bfloat16)
            low = (rest - middle.astype(jnp.float32)).astype(jnp.bfloat16)
            columns = slice(k * LANES, (k + 1) * LANES)
            parts[f, 0:m, columns] = high
            parts[f, m : 2 * m, columns] = middle
            parts[f, 2 * m : 3 * m, columns] = low
        product = lax.dot_general(
            parts[f], parts[f, 0 : 2 * m, :], (((1,), (1,)), ((), ())), preferred_element_type=jnp.float32
        )
        cross = product[2 * m : 3 * m, 0:m]
        gram = (product[m : 2 * m, m : 2 * m] + (cross + cross.T)) + (
            product[0:m, m : 2 * m] + product[m : 2 * m, 0:m]
        )
        grams.append(gram + product[0:m, 0:m])
        projs.append(as_row(jnp.sum(proj, axis=1, keepdims=True), eye))
        own = jnp.where(parity == f, residual * residual, 0.0)
        total = jnp.sum(jnp.sum(own, axis=0, keepdims=True), axis=1, keepdims=True)
        squares.append(jnp.broadcast_to(total, (1, LANES)))
    below = lax.broadcasted_iota(jnp.int32, (m, m), 0) > lax.broadcasted_iota(jnp.int32, (m, m), 1)
    out_ref[0:m, :] = jnp.where(below, grams[0], grams[1])
    diagonal = jnp.sum(jnp.where(eye, grams[0], 0.0), axis=0, keepdims=True)
    at = lax.broadcasted_iota(jnp.int32, (out_ref.shape[0] - m, LANES), 0)
    extra = jnp.zeros(at.shape, jnp.float32)
    for i, row in enumerate((projs[0], projs[1], diagonal, squares[0], squares[1])):
        extra = jnp.where(at == i, row, extra)
    out_ref[m:, :] = extra


def solve_kernel(rows_all, sums_ref, diffs_ref, correction_ref, coefficients_ref, staged, matrix, x, r, p, sem):
    m = diffs_ref.shape[0]
    copy = pltpu.make_async_copy(diffs_ref, staged, sem)
    copy.start()
    eye = eye_mask(m)
    below = lax.broadcasted_iota(jnp.int32, (m, m), 0) > lax.broadcasted_iota(jnp.int32, (m, m), 1)
    packed = sums_ref[0:m, :]
    extra = sums_ref[m : m + 8, :]
    w0 = 1.0 / (extra[3:4, :] / rows_all + EPSILON)
    w1 = 1.0 / (extra[4:5, :] / rows_all + EPSILON)
    turned = packed.T
    gram = jnp.where(below, w0 * packed + w1 * turned, w1 * packed + w0 * turned)
    gram = jnp.where(eye, w1 * packed + w0 * extra[2:3, :], gram)
    b_row = -(w0 * extra[0:1, :] + w1 * extra[1:2, :])
    only = jnp.where(eye, gram, 0.0)
    scale_row = lax.rsqrt(jnp.sum(only, axis=0, keepdims=True))
    scale = lax.rsqrt(jnp.broadcast_to(jnp.sum(only, axis=1, keepdims=True), (m, m)))
    matrix[...] = (scale * gram) * scale_row
    b = as_column(b_row * scale_row, eye)
    x[...] = jnp.zeros((m, m), jnp.float32)
    r[...] = b
    p[...] = b

    def dot(u, v):
        return jnp.sum(u * v, axis=0, keepdims=True)

    def ratio(top, bottom):
        return jnp.where(bottom > 0.0, top / jnp.where(bottom > 0.0, bottom, 1.0), 0.0)

    start = dot(b, b)
    limit = start[0, 0] * (TOLERANCE * TOLERANCE)

    def going(state):
        step, size, _ = state
        return (step < STEPS_MAX) & (size > limit)

    def advance(state):
        step, _, rr = state
        direction = p[...]
        image = jnp.broadcast_to(
            jnp.sum(matrix[...] * as_row(direction, eye), axis=1, keepdims=True), (m, m)
        )
        alpha = ratio(rr, dot(direction, image))
        x[...] += alpha * direction
        rest = r[...] - alpha * image
        r[...] = rest
        after = dot(rest, rest)
        p[...] = rest + ratio(after, rr) * direction
        return step + 1, after[0, 0], after

    _, size, _ = lax.while_loop(going, advance, (0, start[0, 0], start))

    @pl.when(size > limit)
    def _():
        r[...] = b

        @pl.loop(0, m)
        def _(k):
            lane = lax.broadcasted_iota(jnp.int32, (m, m), 1)
            line = lax.broadcasted_iota(jnp.int32, (m, m), 0)
            here = matrix[...]
            row = matrix[pl.ds(k, 1), :]
            value = r[pl.ds(k, 1), :]
            column = jnp.sum(jnp.where(lane == k, here, 0.0), axis=1, keepdims=True)
            pivot = jnp.sum(jnp.where(lane[0:1] == k, row, 0.0), axis=1, keepdims=True)
            factor = jnp.where(line == k, 0.0, column / pivot)
            matrix[...] = here - factor * row
            r[...] = r[...] - factor * value

        x[...] = r[...] / jnp.broadcast_to(
            jnp.sum(jnp.where(eye, matrix[...], 0.0), axis=1, keepdims=True), (m, m)
        )

    found = scale * x[...]
    x[...] = found
    coefficients_ref[...] = as_row(found, eye)
    copy.wait()
    lines = correction_ref.shape[0]
    totals = [jnp.zeros((lines, LANES), jnp.float32) for _ in range(2)]
    for k in range(m):
        totals[k % 2] += staged[k] * x[k : k + 1, :]
    correction_ref[...] = totals[0] + totals[1]


def local_sums(res_diffs, residual, lines):
    m = res_diffs.shape[0]
    diffs = rows_of(res_diffs)
    rows = diffs.shape[1]
    return pl.pallas_call(
        gram_kernel,
        out_shape=jax.ShapeDtypeStruct((lines, LANES), jnp.float32),
        in_specs=[pl.BlockSpec(memory_space=pl.ANY), pl.BlockSpec(memory_space=pltpu.VMEM)],
        out_specs=pl.BlockSpec(memory_space=pltpu.VMEM),
        scratch_shapes=[
            pltpu.VMEM((rows, m, LANES), jnp.float32),
            pltpu.VMEM((2, 3 * m, rows // 2 * LANES), jnp.bfloat16),
            pltpu.SemaphoreType.DMA((rows,)),
        ],
        name="gram",
    )(diffs, rows_of(residual))


def solve_and_apply(sums, out_diffs, rows_all):
    m = out_diffs.shape[0]
    diffs = rows_of(out_diffs)
    lines = diffs.shape[1]
    square = pltpu.VMEM((m, LANES), jnp.float32)
    correction, coefficients = pl.pallas_call(
        lambda *refs: solve_kernel(rows_all, *refs),
        out_shape=(
            jax.ShapeDtypeStruct((lines, LANES), jnp.float32),
            jax.ShapeDtypeStruct((1, m), jnp.float32),
        ),
        in_specs=[pl.BlockSpec(memory_space=pltpu.VMEM), pl.BlockSpec(memory_space=pl.ANY)],
        out_specs=(pl.BlockSpec(memory_space=pltpu.VMEM), pl.BlockSpec(memory_space=pltpu.VMEM)),
        scratch_shapes=[pltpu.VMEM((m, lines, LANES), jnp.float32), square, square, square, square, pltpu.SemaphoreType.DMA],
        name="solve",
    )(sums, diffs)
    fields = out_diffs.shape[1]
    blocks = correction.reshape(lines // fields, fields, LANES)
    return jnp.swapaxes(blocks, 0, 1).reshape(fields, -1), coefficients.reshape(m)


def exchange(chunks, groups):
    return lax.all_to_all(chunks, AXIS, 0, 0, axis_index_groups=groups)


def on_device(res_diffs, out_diffs, residual):
    rows_all = residual.shape[1] * lax.axis_size(AXIS)
    inner = groups_over(INNER)
    outer = groups_over([name for name in BITS if name not in INNER])
    pieces = len(inner[0])
    lines = -(-133 // pieces) * pieces
    sums = local_sums(res_diffs, residual, lines)
    part = jnp.sum(exchange(sums.reshape(pieces, 1, -1), inner), axis=0)
    part = jnp.sum(exchange(jnp.broadcast_to(part, (len(outer[0]),) + part.shape), outer), axis=0)
    whole = exchange(jnp.broadcast_to(part, (pieces,) + part.shape), inner)
    return solve_and_apply(whole.reshape(lines, LANES), out_diffs, rows_all)


def solution(mesh):
    placed = (P(None, None, AXIS), P(None, None, AXIS), P(None, AXIS))
    return jax.shard_map(
        on_device, mesh=mesh, in_specs=placed, out_specs=(P(None, AXIS), P()), check_vma=False
    )
```

time: 416 us -> 60.2 us (0.14)
  waiting for transfers between devices: 158 us -> 0 us
  blocking collectives: 201 us -> 49.8 us
  other arithmetic: 27.5 us -> 0.16 us
  between operations: 14.1 us -> 0.66 us
  matrix products: 11.5 us -> 0 us
  Pallas kernels: 0 us -> 8.96 us
    psum x2 -> x0, blocking collectives: 201 us -> none  [the longest x1 106 us: on_device(): total = lax.psum(squares, 'iface')]
    psum x1 -> x0, waiting for transfers between devices: 158 us -> none  [on_device(): gram, proj = lax.psum((local_gram, local_proj), 'iface')]
    all_to_all x0 -> x3, blocking collectives: none -> 49.8 us  [exchange(): return lax.all_to_all(chunks, AXIS, 0, 0, axis_index_groups=groups)]
    another operation x5 -> x0, other arithmetic: 22.9 us -> none  [the longest x3 12.4 us: on_device(): lower_part = jnp.linalg.cholesky(gram)]
    dot_general x3 -> x0, matrix products: 11.1 us -> none  [the longest x1 4.66 us: on_device(): local_gram = jnp.einsum('mfi,nfi->mn', scaled, scaled, precision=precise)]
    pallas_call x0 -> x2, Pallas kernels: none -> 8.96 us  [the longest x1 5.6 us: local_sums(): pl.pallas_call(gram_kernel, out_shape=jax.ShapeDtypeStruct((lines, LANES)...]
  transfers between devices with their start and end apart: 1 -> 0, of which waited for: 1 -> 0; matrix products, arithmetic and copies ran while one was open for 1% -> 0% of each run, Pallas kernels for 0% -> 0%
where the time goes in v1:
time: 60.2 us; the launch traced here: 59.7 us
  blocking collectives  49.8 us (83%)
  Pallas kernels  8.96 us (15%)
  between operations  0.66 us (1%)
    all_to_all x3, blocking collectives, exchange(): return lax.all_to_all(chunks, AXIS, 0, 0, axis_index_groups=groups)  49.8 us
    pallas_call x1, Pallas kernels, local_sums(): pl.pallas_call(gram_kernel, out_shape=jax.ShapeDtypeStruct((lines, LANES)...  5.6 us
    pallas_call x1, Pallas kernels, solve_and_apply(): pl.pallas_call(lambda *refs: solve_kernel(rows_all, *refs), out_shape=(ja...  3.36 us

profile of v1, /device:TPU:1, one launch (start us, length us, event | category | flops | bytes accessed | tf_op | source)
XLA Modules:
  0.0 59.7 jit_solution(18092693865384773146)
XLA Ops:
  0.6 5.6 %gram.1 = f32[144,128]{1,0:T(8,128)} custom-call(f32[128,32,128]{2,1,0:T(8,128)} %bitcast.23, f32[32,128]{1,0:T(8,128)} %bitcast.27), custom_call_target="tpu_custom_call" | custom-call | tf_op jit(solution)/shard_map/gram/pallas_call | solution.py:185
  6.2 16.0 %all_to_all.15 = f32[16,1,1152]{2,1,0:T(1,128)S(1)} all-to-all(f32[16,1,1152]{2,1,0:T(1,128)} %bitcast.26), channel_id=1, replica_groups={{0,1,2,3,4,5,6,7,64,65,66,67,68,69,70,71},{8,9,10,11,12,13,14,15,72,73,..., dimensions={0} | all-to-all | bytes 147456 | tf_op jit(solution)/shard_map/all_to_all | solution.py:221
  22.3 0.1 reduce_sum.18
  22.3 0.1 broadcast_in_dim.6
  22.4 22.8 %all_to_all.16 = f32[32,1,1152]{2,1,0:T(1,128)S(1)} all-to-all(f32[32,1,1152]{2,1,0:T(1,128)S(1)} %broadcast_in_dim.6), channel_id=1, replica_groups={{0,8,16,24,32,40,48,56,128,136,144,152,160,168,176,184,256,264,272,280,..., dimensions={0} | all-to-all | bytes 294912 | tf_op jit(solution)/shard_map/all_to_all | solution.py:221
  45.2 0.1 reduce_sum.19
  45.3 11.1 %all_to_all.17 = f32[16,1,1152]{2,1,0:T(1,128)} all-to-all(f32[16,1,1152]{2,1,0:T(1,128)S(1)} %broadcast_in_dim.7), channel_id=1, replica_groups={{0,1,2,3,4,5,6,7,64,65,66,67,68,69,70,71},{8,9,10,11,12,13,14,15,72,73,..., dimensions={0} | all-to-all | bytes 147456 | tf_op jit(solution)/shard_map/all_to_all | solution.py:221
  56.4 3.4 %solve.1 = (f32[32,128]{1,0:T(8,128)}, f32[1,128]{1,0:T(1,128)}) custom-call(f32[144,128]{1,0:T(8,128)} %bitcast.25, f32[128,32,128]{2,1,0:T(8,128)} %bitcast.24), custom_call_target="tpu_custom_call" | custom-call | tf_op jit(solution)/shard_map/solve/pallas_call | solution.py:204
  (1 shorter events, 0.0 us)

commit v2 on v1

--- a/solution.py
+++ b/solution.py
@@ -10,7 +10,7 @@
 EPSILON = 1e-06
 TOLERANCE = 1e-06
 STEPS_MAX = 16
-INNER = ("y0", "x1", "x0", "c")
+INNER = ("y0", "z0", "x1", "x0", "c")
 BITS = ("y2", "y1", "y0", "z2", "z1", "z0", "x1", "x0", "c")
 
 
@@ -184,7 +184,7 @@
     rows = diffs.shape[1]
     return pl.pallas_call(
         gram_kernel,
-        out_shape=jax.ShapeDtypeStruct((lines, LANES), jnp.float32),
+        out_shape=pltpu.VMEM((lines, LANES), jnp.float32),
         in_specs=[pl.BlockSpec(memory_space=pl.ANY), pl.BlockSpec(memory_space=pltpu.VMEM)],
         out_specs=pl.BlockSpec(memory_space=pltpu.VMEM),
         scratch_shapes=[
@@ -211,7 +211,7 @@
         out_specs=(pl.BlockSpec(memory_space=pltpu.VMEM), pl.BlockSpec(memory_space=pltpu.VMEM)),
         scratch_shapes=[pltpu.VMEM((m, lines, LANES), jnp.float32), square, square, square, square, pltpu.SemaphoreType.DMA],
         name="solve",
-    )(sums, diffs)
+    )(pltpu.with_memory_space_constraint(sums, pltpu.VMEM), diffs)
     fields = out_diffs.shape[1]
     blocks = correction.reshape(lines // fields, fields, LANES)
     return jnp.swapaxes(blocks, 0, 1).reshape(fields, -1), coefficients.reshape(m)

time: 60.2 us -> 60.1 us (level)
  blocking collectives: 49.8 us -> 51.4 us
  Pallas kernels: 8.96 us -> 7.47 us
    all_to_all x3, blocking collectives: 49.8 us -> 51.4 us  [exchange(): return lax.all_to_all(chunks, AXIS, 0, 0, axis_index_groups=groups)]
    pallas_call x1, Pallas kernels: 3.36 us -> 2.48 us  [solve_and_apply(): pl.pallas_call(lambda *refs: solve_kernel(rows_all, *refs), out_shape=(ja...]
    pallas_call x1, Pallas kernels: 5.6 us -> 4.98 us  [local_sums(): pl.pallas_call(gram_kernel, out_shape=pltpu.VMEM((lines, LANES), jnp.floa...]
where the time goes in v2:
time: 60.1 us; the launch traced here: 59.7 us
  blocking collectives  51.4 us (86%)
  Pallas kernels  7.47 us (12%)
  between operations  0.65 us (1%)
    all_to_all x3, blocking collectives, exchange(): return lax.all_to_all(chunks, AXIS, 0, 0, axis_index_groups=groups)  51.4 us
    pallas_call x1, Pallas kernels, local_sums(): pl.pallas_call(gram_kernel, out_shape=pltpu.VMEM((lines, LANES), jnp.floa...  4.98 us
    pallas_call x1, Pallas kernels, solve_and_apply(): pl.pallas_call(lambda *refs: solve_kernel(rows_all, *refs), out_shape=(ja...  2.48 us

profile of v2, /device:TPU:1, one launch (start us, length us, event | category | flops | bytes accessed | tf_op | source)
XLA Modules:
  0.0 59.7 jit_solution(2351676302065560410)
XLA Ops:
  0.6 5.0 %gram.1 = f32[160,128]{1,0:T(8,128)S(1)} custom-call(f32[128,32,128]{2,1,0:T(8,128)} %bitcast.25, f32[32,128]{1,0:T(8,128)} %bitcast.27), custom_call_target="tpu_custom_call" | custom-call | tf_op jit(solution)/shard_map/gram/pallas_call | solution.py:185
  5.6 16.4 %all_to_all.15 = f32[32,1,640]{2,1,0:T(1,128)S(1)} all-to-all(f32[32,1,640]{2,1,0:T(1,128)S(1)} %bitcast.24), channel_id=1, replica_groups={{0,1,2,3,4,5,6,7,8,9,10,11,12,13,14,15,64,65,66,67,68,69,70,71,72,73,74..., dimensions={0} | all-to-all | bytes 163840 | tf_op jit(solution)/shard_map/all_to_all | solution.py:221
  22.0 0.1 reduce_sum.18
  22.1 23.7 %all_to_all.16 = f32[16,1,640]{2,1,0:T(1,128)S(1)} all-to-all(f32[16,1,640]{2,1,0:T(1,128)S(1)} %broadcast_in_dim.6), channel_id=1, replica_groups={{0,16,32,48,128,144,160,176,256,272,288,304,384,400,416,432},{1,17,33,4..., dimensions={0} | all-to-all | bytes 81920 | tf_op jit(solution)/shard_map/all_to_all | solution.py:221
  45.9 11.4 %all_to_all.17 = f32[32,1,640]{2,1,0:T(1,128)S(1)} all-to-all(f32[32,1,640]{2,1,0:T(1,128)S(1)} %broadcast_in_dim.7), channel_id=1, replica_groups={{0,1,2,3,4,5,6,7,8,9,10,11,12,13,14,15,64,65,66,67,68,69,70,71,72,73,74..., dimensions={0} | all-to-all | bytes 163840 | tf_op jit(solution)/shard_map/all_to_all | solution.py:221
  57.2 2.5 %solve.1 = (f32[32,128]{1,0:T(8,128)}, f32[1,128]{1,0:T(1,128)}) custom-call(f32[160,128]{1,0:T(8,128)S(1)} %bitcast.23, f32[128,32,128]{2,1,0:T(8,128)} %bitcast.26), custom_call_target="tpu_custom_call" | custom-call | tf_op jit(solution)/shard_map/solve/pallas_call | solution.py:204
  (3 shorter events, 0.1 us)

commit v3 on v2

--- a/solution.py
+++ b/solution.py
@@ -7,10 +7,12 @@
 
 AXIS = "iface"
 LANES = 128
+SUBLANES = 8
 EPSILON = 1e-06
 TOLERANCE = 1e-06
 STEPS_MAX = 16
-INNER = ("y0", "z0", "x1", "x0", "c")
+INNER = ('y0', 'x1', 'x0', 'c')
+STEPS = [('y2', 'y1', 'z2', 'z1', 'z0')]
 BITS = ("y2", "y1", "y0", "z2", "z1", "z0", "x1", "x0", "c")
 
 
@@ -44,60 +46,69 @@
     return jnp.broadcast_to(jnp.sum(jnp.where(eye, row, 0.0), axis=1, keepdims=True), (m, m))
 
 
-def gram_kernel(diffs_ref, residual_ref, out_ref, staged, parts, sems):
-    m = diffs_ref.shape[0]
-    rows = diffs_ref.shape[1]
-    order = [*range(0, rows, 2), *range(1, rows, 2)]
-    copies = {}
-    for j in order:
-        copies[j] = pltpu.make_async_copy(diffs_ref.at[:, j, :], staged.at[j], sems.at[j])
-        copies[j].start()
+def split(x):
+    high = x.astype(jnp.bfloat16)
+    rest = x - high.astype(jnp.float32)
+    middle = rest.astype(jnp.bfloat16)
+    return high, middle, (rest - middle.astype(jnp.float32)).astype(jnp.bfloat16)
+
+
+def gram_kernel(diffs_ref, residual_ref, out_ref, staged, sems):
+    m, rows = diffs_ref.shape[:2]
+    tiles = rows // SUBLANES
+    copies = [
+        pltpu.make_async_copy(
+            diffs_ref.at[:, t * SUBLANES : (t + 1) * SUBLANES, :], staged.at[t], sems.at[t]
+        )
+        for t in range(tiles)
+    ]
+    for copy in copies:
+        copy.start()
     eye = eye_mask(m)
     residual = residual_ref[...]
     parity = lax.broadcasted_iota(jnp.int32, residual.shape, 0) & 1
-    grams, projs, squares = [], [], []
+    squares = []
     for f in range(2):
-        proj = None
-        for k in range(rows // 2):
-            j = 2 * k + f
-            copies[j].wait()
-            block = staged[j]
-            term = block * residual_ref[j : j + 1, :]
-            proj = term if proj is None else proj + term
-            high = block.astype(jnp.bfloat16)
-            rest = block - high.astype(jnp.float32)
-            middle = rest.astype(jnp.bfloat16)
-            low = (rest - middle.astype(jnp.float32)).astype(jnp.bfloat16)
-            columns = slice(k * LANES, (k + 1) * LANES)
-            parts[f, 0:m, columns] = high
-            parts[f, m : 2 * m, columns] = middle
-            parts[f, 2 * m : 3 * m, columns] = low
-        product = lax.dot_general(
-            parts[f], parts[f, 0 : 2 * m, :], (((1,), (1,)), ((), ())), preferred_element_type=jnp.float32
-        )
-        cross = product[2 * m : 3 * m, 0:m]
-        gram = (product[m : 2 * m, m : 2 * m] + (cross + cross.T)) + (
-            product[0:m, m : 2 * m] + product[m : 2 * m, 0:m]
-        )
-        grams.append(gram + product[0:m, 0:m])
-        projs.append(as_row(jnp.sum(proj, axis=1, keepdims=True), eye))
         own = jnp.where(parity == f, residual * residual, 0.0)
         total = jnp.sum(jnp.sum(own, axis=0, keepdims=True), axis=1, keepdims=True)
         squares.append(jnp.broadcast_to(total, (1, LANES)))
+    projs = [jnp.zeros((m, LANES), jnp.float32)] * 2
+    products = [jnp.zeros((3 * m, 2 * m), jnp.float32)] * 2
+    for t in range(tiles):
+        copies[t].wait()
+        lines = staged.at[t].reshape(m * SUBLANES, LANES)
+        for f in range(2):
+            parts = []
+            for s in range(f, SUBLANES, 2):
+                block = lines[pl.ds(s, m, stride=SUBLANES), :]
+                row = t * SUBLANES + s
+                projs[f] = projs[f] + block * residual_ref[row : row + 1, :]
+                parts.append(split(block))
+            high, middle, low = (jnp.concatenate(part, axis=1) for part in zip(*parts))
+            products[f] = products[f] + lax.dot_general(
+                jnp.concatenate([high, middle, low], axis=0),
+                jnp.concatenate([high, middle], axis=0),
+                (((1,), (1,)), ((), ())),
+                preferred_element_type=jnp.float32,
+            )
+    grams = []
+    for product in products:
+        cross = product[2 * m :, 0:m]
+        small = product[m : 2 * m, m:] + (cross + cross.T)
+        grams.append(product[0:m, 0:m] + (small + (product[0:m, m:] + product[m : 2 * m, 0:m])))
     below = lax.broadcasted_iota(jnp.int32, (m, m), 0) > lax.broadcasted_iota(jnp.int32, (m, m), 1)
     out_ref[0:m, :] = jnp.where(below, grams[0], grams[1])
-    diagonal = jnp.sum(jnp.where(eye, grams[0], 0.0), axis=0, keepdims=True)
+    lines = [as_row(jnp.sum(proj, axis=1, keepdims=True), eye) for proj in projs]
+    lines += [as_row(grams[0], eye), *squares]
     at = lax.broadcasted_iota(jnp.int32, (out_ref.shape[0] - m, LANES), 0)
     extra = jnp.zeros(at.shape, jnp.float32)
-    for i, row in enumerate((projs[0], projs[1], diagonal, squares[0], squares[1])):
-        extra = jnp.where(at == i, row, extra)
+    for i, line in enumerate(lines):
+        extra = jnp.where(at == i, line, extra)
     out_ref[m:, :] = extra
 
 
-def solve_kernel(rows_all, sums_ref, diffs_ref, correction_ref, coefficients_ref, staged, matrix, x, r, p, sem):
+def solve_kernel(rows_all, sums_ref, diffs_ref, correction_ref, coefficients_ref, matrix, x, r, p):
     m = diffs_ref.shape[0]
-    copy = pltpu.make_async_copy(diffs_ref, staged, sem)
-    copy.start()
     eye = eye_mask(m)
     below = lax.broadcasted_iota(jnp.int32, (m, m), 0) > lax.broadcasted_iota(jnp.int32, (m, m), 1)
     packed = sums_ref[0:m, :]
@@ -170,11 +181,10 @@
     found = scale * x[...]
     x[...] = found
     coefficients_ref[...] = as_row(found, eye)
-    copy.wait()
     lines = correction_ref.shape[0]
     totals = [jnp.zeros((lines, LANES), jnp.float32) for _ in range(2)]
     for k in range(m):
-        totals[k % 2] += staged[k] * x[k : k + 1, :]
+        totals[k % 2] += diffs_ref[k] * x[k : k + 1, :]
     correction_ref[...] = totals[0] + totals[1]
 
 
@@ -188,18 +198,15 @@
         in_specs=[pl.BlockSpec(memory_space=pl.ANY), pl.BlockSpec(memory_space=pltpu.VMEM)],
         out_specs=pl.BlockSpec(memory_space=pltpu.VMEM),
         scratch_shapes=[
-            pltpu.VMEM((rows, m, LANES), jnp.float32),
-            pltpu.VMEM((2, 3 * m, rows // 2 * LANES), jnp.bfloat16),
-            pltpu.SemaphoreType.DMA((rows,)),
+            pltpu.VMEM((rows // SUBLANES, m, SUBLANES, LANES), jnp.float32),
+            pltpu.SemaphoreType.DMA((rows // SUBLANES,)),
         ],
         name="gram",
     )(diffs, rows_of(residual))
 
 
-def solve_and_apply(sums, out_diffs, rows_all):
-    m = out_diffs.shape[0]
-    diffs = rows_of(out_diffs)
-    lines = diffs.shape[1]
+def solve_and_apply(sums, diffs, rows_all):
+    m, lines = diffs.shape[:2]
     square = pltpu.VMEM((m, LANES), jnp.float32)
     correction, coefficients = pl.pallas_call(
         lambda *refs: solve_kernel(rows_all, *refs),
@@ -207,14 +214,13 @@
             jax.ShapeDtypeStruct((lines, LANES), jnp.float32),
             jax.ShapeDtypeStruct((1, m), jnp.float32),
         ),
-        in_specs=[pl.BlockSpec(memory_space=pltpu.VMEM), pl.BlockSpec(memory_space=pl.ANY)],
+        in_specs=[pl.BlockSpec(memory_space=pltpu.VMEM), pl.BlockSpec(memory_space=pltpu.VMEM)],
         out_specs=(pl.BlockSpec(memory_space=pltpu.VMEM), pl.BlockSpec(memory_space=pltpu.VMEM)),
-        scratch_shapes=[pltpu.VMEM((m, lines, LANES), jnp.float32), square, square, square, square, pltpu.SemaphoreType.DMA],
+        scratch_shapes=[square, square, square, square],
         name="solve",
     )(pltpu.with_memory_space_constraint(sums, pltpu.VMEM), diffs)
-    fields = out_diffs.shape[1]
-    blocks = correction.reshape(lines // fields, fields, LANES)
-    return jnp.swapaxes(blocks, 0, 1).reshape(fields, -1), coefficients.reshape(m)
+    blocks = correction.reshape(lines // 2, 2, LANES)
+    return jnp.swapaxes(blocks, 0, 1).reshape(2, -1), coefficients.reshape(m)
 
 
 def exchange(chunks, groups):
@@ -224,14 +230,17 @@
 def on_device(res_diffs, out_diffs, residual):
     rows_all = residual.shape[1] * lax.axis_size(AXIS)
     inner = groups_over(INNER)
-    outer = groups_over([name for name in BITS if name not in INNER])
     pieces = len(inner[0])
     lines = -(-133 // pieces) * pieces
     sums = local_sums(res_diffs, residual, lines)
+    sums, out_diffs = lax.optimization_barrier((sums, out_diffs))
+    fetched = pltpu.with_memory_space_constraint(rows_of(out_diffs), pltpu.VMEM)
     part = jnp.sum(exchange(sums.reshape(pieces, 1, -1), inner), axis=0)
-    part = jnp.sum(exchange(jnp.broadcast_to(part, (len(outer[0]),) + part.shape), outer), axis=0)
+    for names in STEPS:
+        groups = groups_over(names)
+        part = jnp.sum(exchange(jnp.broadcast_to(part, (len(groups[0]),) + part.shape), groups), axis=0)
     whole = exchange(jnp.broadcast_to(part, (pieces,) + part.shape), inner)
-    return solve_and_apply(whole.reshape(lines, LANES), out_diffs, rows_all)
+    return solve_and_apply(whole.reshape(lines, LANES), fetched, rows_all)
 
 
 def solution(mesh):

time: 60.1 us -> 56.1 us (0.933)
  blocking collectives: 51.4 us -> 49.1 us
  Pallas kernels: 7.47 us -> 5.81 us
    all_to_all x3, blocking collectives: 51.4 us -> 49.1 us  [exchange(): return lax.all_to_all(chunks, AXIS, 0, 0, axis_index_groups=groups)]
    pallas_call x1, Pallas kernels: 4.98 us -> 3.57 us  [local_sums(): pl.pallas_call(gram_kernel, out_shape=pltpu.VMEM((lines, LANES), jnp.floa...]
where the time goes in v3:
time: 56.1 us; the launch traced here: 55.8 us
  blocking collectives  49.1 us (88%)
  Pallas kernels  5.81 us (10%)
  between operations  0.67 us (1%)
    all_to_all x3, blocking collectives, exchange(): return lax.all_to_all(chunks, AXIS, 0, 0, axis_index_groups=groups)  49.1 us
    pallas_call x1, Pallas kernels, local_sums(): pl.pallas_call(gram_kernel, out_shape=pltpu.VMEM((lines, LANES), jnp.floa...  3.57 us
    pallas_call x1, Pallas kernels, solve_and_apply(): pl.pallas_call(lambda *refs: solve_kernel(rows_all, *refs), out_shape=(ja...  2.24 us

profile of v3, /device:TPU:1, one launch (start us, length us, event | category | flops | bytes accessed | tf_op | source)
XLA Modules:
  0.0 55.8 jit_solution(2363581886230450549)
XLA Ops:
  0.6 0.0 copy-start
  0.6 3.6 %gram.1 = f32[144,128]{1,0:T(8,128)S(1)} custom-call(f32[128,32,128]{2,1,0:T(8,128)} %bitcast.26, f32[32,128]{1,0:T(8,128)} %bitcast.27), custom_call_target="tpu_custom_call" | custom-call | tf_op jit(solution)/shard_map/gram/pallas_call | solution.py:195
  4.2 15.1 %all_to_all.15 = f32[16,1,1152]{2,1,0:T(1,128)S(1)} all-to-all(f32[16,1,1152]{2,1,0:T(1,128)S(1)} %bitcast.25), channel_id=1, replica_groups={{0,1,2,3,4,5,6,7,64,65,66,67,68,69,70,71},{8,9,10,11,12,13,14,15,72,73,..., dimensions={0} | all-to-all | bytes 147456 | tf_op jit(solution)/shard_map/all_to_all | solution.py:227
  19.4 0.1 reduce_sum.18
  19.4 0.1 broadcast_in_dim.6
  19.5 23.4 %all_to_all.16 = f32[32,1,1152]{2,1,0:T(1,128)S(1)} all-to-all(f32[32,1,1152]{2,1,0:T(1,128)S(1)} %broadcast_in_dim.6), channel_id=1, replica_groups={{0,8,16,24,32,40,48,56,128,136,144,152,160,168,176,184,256,264,272,280,..., dimensions={0} | all-to-all | bytes 294912 | tf_op jit(solution)/shard_map/all_to_all | solution.py:227
  42.9 0.1 reduce_sum.19
  43.1 10.5 %all_to_all.17 = f32[16,1,1152]{2,1,0:T(1,128)S(1)} all-to-all(f32[16,1,1152]{2,1,0:T(1,128)S(1)} %broadcast_in_dim.7), channel_id=1, replica_groups={{0,1,2,3,4,5,6,7,64,65,66,67,68,69,70,71},{8,9,10,11,12,13,14,15,72,73,..., dimensions={0} | all-to-all | bytes 147456 | tf_op jit(solution)/shard_map/all_to_all | solution.py:227
  53.6 0.0 copy-done
  53.6 2.2 %solve.1 = (f32[32,128]{1,0:T(8,128)}, f32[1,128]{1,0:T(1,128)}) custom-call(f32[144,128]{1,0:T(8,128)S(1)} %bitcast.24, f32[128,32,128]{2,1,0:T(8,128)S(1)} %bitcast.23), custom_call_target="tpu_custom_call" | custom-call | tf_op jit(solution)/shard_map/solve/pallas_call | solution.py:211
  (1 shorter events, 0.0 us)
Async XLA Ops:
  0.6 52.9 %copy-start = (f32[128,2,2048]{2,1,0:T(2,128)S(1)}, f32[128,2,2048]{2,1,0:T(2,128)}, u32[]{:S(2)}) copy-start(f32[128,2,2048]{2,1,0:T(2,128)} %param.4) | copy-start | bytes 6291460

commit v4 on v3

--- a/solution.py
+++ b/solution.py
@@ -13,17 +13,19 @@
 STEPS_MAX = 16
 INNER = ('y0', 'x1', 'x0', 'c')
 STEPS = [('y2', 'y1', 'z2', 'z1', 'z0')]
+ROOT = ('y0', 'x1', 'y2', 'z2')
 BITS = ("y2", "y1", "y0", "z2", "z1", "z0", "x1", "x0", "c")
 
 
 def groups_over(names):
     count = len(BITS)
+    root = sum(1 << (count - 1 - BITS.index(name)) for name in names if name in ROOT)
     found = {}
     for device in range(1 << count):
-        bits = [(device >> (count - 1 - k)) & 1 for k in range(count)]
+        bits = [((device ^ root) >> (count - 1 - k)) & 1 for k in range(count)]
         key = tuple(b for b, name in zip(bits, BITS) if name not in names)
         found.setdefault(key, []).append(device)
-    return list(found.values())
+    return [sorted(group, key=lambda device: device ^ root) for group in found.values()]
 
 
 def rows_of(x):
@@ -53,9 +55,11 @@
     return high, middle, (rest - middle.astype(jnp.float32)).astype(jnp.bfloat16)
 
 
-def gram_kernel(diffs_ref, residual_ref, out_ref, staged, sems):
+def gram_kernel(diffs_ref, given_ref, out_ref, staged, residual_ref, sems):
     m, rows = diffs_ref.shape[:2]
     tiles = rows // SUBLANES
+    first = pltpu.make_async_copy(given_ref, residual_ref, sems.at[tiles])
+    first.start()
     copies = [
         pltpu.make_async_copy(
             diffs_ref.at[:, t * SUBLANES : (t + 1) * SUBLANES, :], staged.at[t], sems.at[t]
@@ -65,6 +69,7 @@
     for copy in copies:
         copy.start()
     eye = eye_mask(m)
+    first.wait()
     residual = residual_ref[...]
     parity = lax.broadcasted_iota(jnp.int32, residual.shape, 0) & 1
     squares = []
@@ -195,11 +200,12 @@
     return pl.pallas_call(
         gram_kernel,
         out_shape=pltpu.VMEM((lines, LANES), jnp.float32),
-        in_specs=[pl.BlockSpec(memory_space=pl.ANY), pl.BlockSpec(memory_space=pltpu.VMEM)],
+        in_specs=[pl.BlockSpec(memory_space=pl.ANY), pl.BlockSpec(memory_space=pl.ANY)],
         out_specs=pl.BlockSpec(memory_space=pltpu.VMEM),
         scratch_shapes=[
             pltpu.VMEM((rows // SUBLANES, m, SUBLANES, LANES), jnp.float32),
-            pltpu.SemaphoreType.DMA((rows // SUBLANES,)),
+            pltpu.VMEM((rows, LANES), jnp.float32),
+            pltpu.SemaphoreType.DMA((rows // SUBLANES + 1,)),
         ],
         name="gram",
     )(diffs, rows_of(residual))

time: 56.1 us -> 48.4 us (0.86)
  blocking collectives: 49.1 us -> 42.1 us
  Pallas kernels: 5.81 us -> 5.13 us
    all_to_all x3, blocking collectives: 49.1 us -> 42.1 us  [exchange(): return lax.all_to_all(chunks, AXIS, 0, 0, axis_index_groups=groups)]
    pallas_call x1, Pallas kernels: 3.57 us -> 2.89 us  [local_sums(): pl.pallas_call(gram_kernel, out_shape=pltpu.VMEM((lines, LANES), jnp.floa...]
where the time goes in v4:
time: 48.4 us; the launch traced here: 48.2 us
  blocking collectives  42.1 us (87%)
  Pallas kernels  5.13 us (11%)
  between operations  0.67 us (1%)
    all_to_all x3, blocking collectives, exchange(): return lax.all_to_all(chunks, AXIS, 0, 0, axis_index_groups=groups)  42.1 us
    pallas_call x1, Pallas kernels, local_sums(): pl.pallas_call(gram_kernel, out_shape=pltpu.VMEM((lines, LANES), jnp.floa...  2.89 us
    pallas_call x1, Pallas kernels, solve_and_apply(): pl.pallas_call(lambda *refs: solve_kernel(rows_all, *refs), out_shape=(ja...  2.24 us

profile of v4, /device:TPU:1, one launch (start us, length us, event | category | flops | bytes accessed | tf_op | source)
XLA Modules:
  0.0 48.2 jit_solution(7523220659437881189)
XLA Ops:
  0.6 0.0 copy-start
  0.6 2.9 %gram.1 = f32[144,128]{1,0:T(8,128)S(1)} custom-call(f32[128,32,128]{2,1,0:T(8,128)} %bitcast.26, f32[32,128]{1,0:T(8,128)} %bitcast.27), custom_call_target="tpu_custom_call" | custom-call | tf_op jit(solution)/shard_map/gram/pallas_call | solution.py:200
  3.5 14.5 %all_to_all.15 = f32[16,1,1152]{2,1,0:T(1,128)S(1)} all-to-all(f32[16,1,1152]{2,1,0:T(1,128)S(1)} %bitcast.25), channel_id=1, replica_groups={{68,69,70,71,64,65,66,67,4,5,6,7,0,1,2,3},{76,77,78,79,72,73,74,75,12,1..., dimensions={0} | all-to-all | bytes 147456 | tf_op jit(solution)/shard_map/all_to_all | solution.py:233
  18.1 0.1 reduce_sum.18
  18.1 0.1 broadcast_in_dim.6
  18.2 18.4 %all_to_all.16 = f32[32,1,1152]{2,1,0:T(1,128)S(1)} all-to-all(f32[32,1,1152]{2,1,0:T(1,128)S(1)} %broadcast_in_dim.6), channel_id=1, replica_groups={{288,296,304,312,256,264,272,280,416,424,432,440,384,392,400,408,32,40,..., dimensions={0} | all-to-all | bytes 294912 | tf_op jit(solution)/shard_map/all_to_all | solution.py:233
  36.6 0.1 reduce_sum.19
  36.8 9.2 %all_to_all.17 = f32[16,1,1152]{2,1,0:T(1,128)S(1)} all-to-all(f32[16,1,1152]{2,1,0:T(1,128)S(1)} %broadcast_in_dim.7), channel_id=1, replica_groups={{68,69,70,71,64,65,66,67,4,5,6,7,0,1,2,3},{76,77,78,79,72,73,74,75,12,1..., dimensions={0} | all-to-all | bytes 147456 | tf_op jit(solution)/shard_map/all_to_all | solution.py:233
  45.9 0.0 copy-done
  45.9 2.2 %solve.1 = (f32[32,128]{1,0:T(8,128)}, f32[1,128]{1,0:T(1,128)}) custom-call(f32[144,128]{1,0:T(8,128)S(1)} %bitcast.24, f32[128,32,128]{2,1,0:T(8,128)S(1)} %bitcast.23), custom_call_target="tpu_custom_call" | custom-call | tf_op jit(solution)/shard_map/solve/pallas_call | solution.py:217
  (1 shorter events, 0.0 us)
Async XLA Ops:
  0.6 45.3 %copy-start = (f32[128,2,2048]{2,1,0:T(2,128)S(1)}, f32[128,2,2048]{2,1,0:T(2,128)}, u32[]{:S(2)}) copy-start(f32[128,2,2048]{2,1,0:T(2,128)} %param.4) | copy-start | bytes 6291460

commit v5 on v4

--- a/solution.py
+++ b/solution.py
@@ -11,9 +11,9 @@
 EPSILON = 1e-06
 TOLERANCE = 1e-06
 STEPS_MAX = 16
-INNER = ('y0', 'x1', 'x0', 'c')
-STEPS = [('y2', 'y1', 'z2', 'z1', 'z0')]
-ROOT = ('y0', 'x1', 'y2', 'z2')
+INNER = ('z0', 'x1', 'x0', 'c')
+STEPS = [('y2', 'y1', 'y0', 'z2', 'z1')]
+ROOT = ('z0', 'x1', 'c', 'y2', 'z2')
 BITS = ("y2", "y1", "y0", "z2", "z1", "z0", "x1", "x0", "c")
 
 
@@ -25,7 +25,7 @@
         bits = [((device ^ root) >> (count - 1 - k)) & 1 for k in range(count)]
         key = tuple(b for b, name in zip(bits, BITS) if name not in names)
         found.setdefault(key, []).append(device)
-    return [sorted(group, key=lambda device: device ^ root) for group in found.values()]
+    return [[group[0] ^ root] + [d for d in group if d != group[0] ^ root] for group in map(sorted, found.values())]
 
 
 def rows_of(x):

time: 48.4 us -> 46.7 us (0.965)
  blocking collectives: 42.1 us -> 40.4 us
    all_to_all x3, blocking collectives: 42.1 us -> 40.4 us  [exchange(): return lax.all_to_all(chunks, AXIS, 0, 0, axis_index_groups=groups)]
where the time goes in v5:
time: 46.7 us; the launch traced here: 46.5 us
  blocking collectives  40.4 us (87%)
  Pallas kernels  5.13 us (11%)
  between operations  0.67 us (1%)
    all_to_all x3, blocking collectives, exchange(): return lax.all_to_all(chunks, AXIS, 0, 0, axis_index_groups=groups)  40.4 us
    pallas_call x1, Pallas kernels, local_sums(): pl.pallas_call(gram_kernel, out_shape=pltpu.VMEM((lines, LANES), jnp.floa...  2.89 us
    pallas_call x1, Pallas kernels, solve_and_apply(): pl.pallas_call(lambda *refs: solve_kernel(rows_all, *refs), out_shape=(ja...  2.24 us

profile of v5, /device:TPU:1, one launch (start us, length us, event | category | flops | bytes accessed | tf_op | source)
XLA Modules:
  0.0 46.5 jit_solution(17198549957711866816)
XLA Ops:
  0.6 0.0 copy-start
  0.6 2.9 %gram.1 = f32[144,128]{1,0:T(8,128)S(1)} custom-call(f32[128,32,128]{2,1,0:T(8,128)} %bitcast.26, f32[32,128]{1,0:T(8,128)} %bitcast.27), custom_call_target="tpu_custom_call" | custom-call | tf_op jit(solution)/shard_map/gram/pallas_call | solution.py:200
  3.5 14.2 %all_to_all.15 = f32[16,1,1152]{2,1,0:T(1,128)S(1)} all-to-all(f32[16,1,1152]{2,1,0:T(1,128)S(1)} %bitcast.25), channel_id=1, replica_groups={{13,0,1,2,3,4,5,6,7,8,9,10,11,12,14,15},{29,16,17,18,19,20,21,22,23,24,..., dimensions={0} | all-to-all | bytes 147456 | tf_op jit(solution)/shard_map/all_to_all | solution.py:233
  17.8 0.1 reduce_sum.18
  17.8 0.1 broadcast_in_dim.6
  17.9 17.2 %all_to_all.16 = f32[32,1,1152]{2,1,0:T(1,128)S(1)} all-to-all(f32[32,1,1152]{2,1,0:T(1,128)S(1)} %broadcast_in_dim.6), channel_id=1, replica_groups={{288,0,16,32,48,64,80,96,112,128,144,160,176,192,208,224,240,256,272,30..., dimensions={0} | all-to-all | bytes 294912 | tf_op jit(solution)/shard_map/all_to_all | solution.py:233
  35.2 0.1 reduce_sum.19
  35.3 8.9 %all_to_all.17 = f32[16,1,1152]{2,1,0:T(1,128)S(1)} all-to-all(f32[16,1,1152]{2,1,0:T(1,128)S(1)} %broadcast_in_dim.7), channel_id=1, replica_groups={{13,0,1,2,3,4,5,6,7,8,9,10,11,12,14,15},{29,16,17,18,19,20,21,22,23,24,..., dimensions={0} | all-to-all | bytes 147456 | tf_op jit(solution)/shard_map/all_to_all | solution.py:233
  44.3 0.0 copy-done
  44.3 2.2 %solve.1 = (f32[32,128]{1,0:T(8,128)}, f32[1,128]{1,0:T(1,128)}) custom-call(f32[144,128]{1,0:T(8,128)S(1)} %bitcast.24, f32[128,32,128]{2,1,0:T(8,128)S(1)} %bitcast.23), custom_call_target="tpu_custom_call" | custom-call | tf_op jit(solution)/shard_map/solve/pallas_call | solution.py:217
  (1 shorter events, 0.0 us)
Async XLA Ops:
  0.6 43.6 %copy-start = (f32[128,2,2048]{2,1,0:T(2,128)S(1)}, f32[128,2,2048]{2,1,0:T(2,128)}, u32[]{:S(2)}) copy-start(f32[128,2,2048]{2,1,0:T(2,128)} %param.4) | copy-start | bytes 6291460

commit v6 on v5

--- a/solution.py
+++ b/solution.py
@@ -10,7 +10,8 @@
 SUBLANES = 8
 EPSILON = 1e-06
 TOLERANCE = 1e-06
-STEPS_MAX = 16
+STEPS_PER_TEST = 4
+TESTS_MAX = 4
 INNER = ('z0', 'x1', 'x0', 'c')
 STEPS = [('y2', 'y1', 'y0', 'z2', 'z1')]
 ROOT = ('z0', 'x1', 'c', 'y2', 'z2')
@@ -55,7 +56,7 @@
     return high, middle, (rest - middle.astype(jnp.float32)).astype(jnp.bfloat16)
 
 
-def gram_kernel(diffs_ref, given_ref, out_ref, staged, residual_ref, sems):
+def gram_kernel(diffs_ref, given_ref, out_ref, staged, residual_ref, products, sems):
     m, rows = diffs_ref.shape[:2]
     tiles = rows // SUBLANES
     first = pltpu.make_async_copy(given_ref, residual_ref, sems.at[tiles])
@@ -78,7 +79,6 @@
         total = jnp.sum(jnp.sum(own, axis=0, keepdims=True), axis=1, keepdims=True)
         squares.append(jnp.broadcast_to(total, (1, LANES)))
     projs = [jnp.zeros((m, LANES), jnp.float32)] * 2
-    products = [jnp.zeros((3 * m, 2 * m), jnp.float32)] * 2
     for t in range(tiles):
         copies[t].wait()
         lines = staged.at[t].reshape(m * SUBLANES, LANES)
@@ -90,14 +90,16 @@
                 projs[f] = projs[f] + block * residual_ref[row : row + 1, :]
                 parts.append(split(block))
             high, middle, low = (jnp.concatenate(part, axis=1) for part in zip(*parts))
-            products[f] = products[f] + lax.dot_general(
+            product = lax.dot_general(
                 jnp.concatenate([high, middle, low], axis=0),
                 jnp.concatenate([high, middle], axis=0),
                 (((1,), (1,)), ((), ())),
                 preferred_element_type=jnp.float32,
             )
+            products[f] = product if t == 0 else products[f] + product
     grams = []
-    for product in products:
+    for f in range(2):
+        product = products[f]
         cross = product[2 * m :, 0:m]
         small = product[m : 2 * m, m:] + (cross + cross.T)
         grams.append(product[0:m, 0:m] + (small + (product[0:m, m:] + product[m : 2 * m, 0:m])))
@@ -140,29 +142,31 @@
         return jnp.where(bottom > 0.0, top / jnp.where(bottom > 0.0, bottom, 1.0), 0.0)
 
     start = dot(b, b)
-    limit = start[0, 0] * (TOLERANCE * TOLERANCE)
-
-    def going(state):
-        step, size, _ = state
-        return (step < STEPS_MAX) & (size > limit)
-
-    def advance(state):
-        step, _, rr = state
-        direction = p[...]
-        image = jnp.broadcast_to(
-            jnp.sum(matrix[...] * as_row(direction, eye), axis=1, keepdims=True), (m, m)
-        )
-        alpha = ratio(rr, dot(direction, image))
-        x[...] += alpha * direction
-        rest = r[...] - alpha * image
-        r[...] = rest
-        after = dot(rest, rest)
-        p[...] = rest + ratio(after, rr) * direction
-        return step + 1, after[0, 0], after
-
-    _, size, _ = lax.while_loop(going, advance, (0, start[0, 0], start))
-
-    @pl.when(size > limit)
+    limit = start * (TOLERANCE * TOLERANCE)
+
+    def advance(rr):
+        for _ in range(STEPS_PER_TEST):
+            direction = p[...]
+            image = jnp.broadcast_to(
+                jnp.sum(matrix[...] * as_row(direction, eye), axis=1, keepdims=True), (m, m)
+            )
+            alpha = ratio(rr, dot(direction, image))
+            x[...] += alpha * direction
+            rest = r[...] - alpha * image
+            r[...] = rest
+            after = dot(rest, rest)
+            p[...] = rest + ratio(after, rr) * direction
+            rr = after
+        return (rr - limit)[0, 0], rr
+
+    over, rr = advance(start)
+    _, over, _ = lax.while_loop(
+        lambda state: (state[0] < TESTS_MAX) & (state[1] > 0.0),
+        lambda state: (state[0] + 1, *advance(state[2])),
+        (1, over, rr),
+    )
+
+    @pl.when(over > 0.0)
     def _():
         r[...] = b
 
@@ -205,6 +209,7 @@
         scratch_shapes=[
             pltpu.VMEM((rows // SUBLANES, m, SUBLANES, LANES), jnp.float32),
             pltpu.VMEM((rows, LANES), jnp.float32),
+            pltpu.VMEM((2, 3 * m, 2 * m), jnp.float32),
             pltpu.SemaphoreType.DMA((rows // SUBLANES + 1,)),
         ],
         name="gram",

time: 46.7 us -> 46.8 us (level)
  no operation moved by 1% of the time
where the time goes in v6:
time: 46.8 us; the launch traced here: 46.6 us
  blocking collectives  40.4 us (86%)
  Pallas kernels  5.18 us (11%)
  between operations  0.67 us (1%)
    all_to_all x3, blocking collectives, exchange(): return lax.all_to_all(chunks, AXIS, 0, 0, axis_index_groups=groups)  40.4 us
    pallas_call x1, Pallas kernels, local_sums(): pl.pallas_call(gram_kernel, out_shape=pltpu.VMEM((lines, LANES), jnp.floa...  2.83 us
    pallas_call x1, Pallas kernels, solve_and_apply(): pl.pallas_call(lambda *refs: solve_kernel(rows_all, *refs), out_shape=(ja...  2.35 us

profile of v6, /device:TPU:1, one launch (start us, length us, event | category | flops | bytes accessed | tf_op | source)
XLA Modules:
  0.0 46.6 jit_solution(4135914712831542961)
XLA Ops:
  0.6 0.0 copy-start
  0.6 2.8 %gram.1 = f32[144,128]{1,0:T(8,128)S(1)} custom-call(f32[128,32,128]{2,1,0:T(8,128)} %bitcast.26, f32[32,128]{1,0:T(8,128)} %bitcast.27), custom_call_target="tpu_custom_call" | custom-call | tf_op jit(solution)/shard_map/gram/pallas_call | solution.py:204
  3.5 14.2 %all_to_all.15 = f32[16,1,1152]{2,1,0:T(1,128)S(1)} all-to-all(f32[16,1,1152]{2,1,0:T(1,128)S(1)} %bitcast.25), channel_id=1, replica_groups={{13,0,1,2,3,4,5,6,7,8,9,10,11,12,14,15},{29,16,17,18,19,20,21,22,23,24,..., dimensions={0} | all-to-all | bytes 147456 | tf_op jit(solution)/shard_map/all_to_all | solution.py:238
  17.7 0.1 reduce_sum.18
  17.8 0.1 broadcast_in_dim.6
  17.9 17.3 %all_to_all.16 = f32[32,1,1152]{2,1,0:T(1,128)S(1)} all-to-all(f32[32,1,1152]{2,1,0:T(1,128)S(1)} %broadcast_in_dim.6), channel_id=1, replica_groups={{288,0,16,32,48,64,80,96,112,128,144,160,176,192,208,224,240,256,272,30..., dimensions={0} | all-to-all | bytes 294912 | tf_op jit(solution)/shard_map/all_to_all | solution.py:238
  35.1 0.1 reduce_sum.19
  35.3 9.0 %all_to_all.17 = f32[16,1,1152]{2,1,0:T(1,128)S(1)} all-to-all(f32[16,1,1152]{2,1,0:T(1,128)S(1)} %broadcast_in_dim.7), channel_id=1, replica_groups={{13,0,1,2,3,4,5,6,7,8,9,10,11,12,14,15},{29,16,17,18,19,20,21,22,23,24,..., dimensions={0} | all-to-all | bytes 147456 | tf_op jit(solution)/shard_map/all_to_all | solution.py:238
  44.2 0.0 copy-done
  44.2 2.4 %solve.1 = (f32[32,128]{1,0:T(8,128)}, f32[1,128]{1,0:T(1,128)}) custom-call(f32[144,128]{1,0:T(8,128)S(1)} %bitcast.24, f32[128,32,128]{2,1,0:T(8,128)S(1)} %bitcast.23), custom_call_target="tpu_custom_call" | custom-call | tf_op jit(solution)/shard_map/solve/pallas_call | solution.py:222
  (1 shorter events, 0.0 us)
Async XLA Ops:
  0.6 43.6 %copy-start = (f32[128,2,2048]{2,1,0:T(2,128)S(1)}, f32[128,2,2048]{2,1,0:T(2,128)}, u32[]{:S(2)}) copy-start(f32[128,2,2048]{2,1,0:T(2,128)} %param.4) | copy-start | bytes 6291460

commit v7 on v6

--- a/solution.py
+++ b/solution.py
@@ -12,9 +12,9 @@
 TOLERANCE = 1e-06
 STEPS_PER_TEST = 4
 TESTS_MAX = 4
-INNER = ('z0', 'x1', 'x0', 'c')
-STEPS = [('y2', 'y1', 'y0', 'z2', 'z1')]
-ROOT = ('z0', 'x1', 'c', 'y2', 'z2')
+INNER = ('y0', 'z0', 'x1', 'x0', 'c')
+STEPS = [('y2', 'y1', 'z2', 'z1')]
+ROOT = ('y0', 'z0', 'x1', 'c', 'y2', 'z2')
 BITS = ("y2", "y1", "y0", "z2", "z1", "z0", "x1", "x0", "c")
 
 
@@ -145,18 +145,19 @@
     limit = start * (TOLERANCE * TOLERANCE)
 
     def advance(rr):
+        held, rest, direction = x[...], r[...], p[...]
         for _ in range(STEPS_PER_TEST):
-            direction = p[...]
+            rr = dot(rest, rest)
             image = jnp.broadcast_to(
                 jnp.sum(matrix[...] * as_row(direction, eye), axis=1, keepdims=True), (m, m)
             )
             alpha = ratio(rr, dot(direction, image))
-            x[...] += alpha * direction
-            rest = r[...] - alpha * image
-            r[...] = rest
-            after = dot(rest, rest)
-            p[...] = rest + ratio(after, rr) * direction
-            rr = after
+            after = rr - alpha * (2.0 * dot(rest, image) - alpha * dot(image, image))
+            held = held + alpha * direction
+            rest = rest - alpha * image
+            direction = rest + ratio(jnp.maximum(after, 0.0), rr) * direction
+        x[...], r[...], p[...] = held, rest, direction
+        rr = dot(rest, rest)
         return (rr - limit)[0, 0], rr
 
     over, rr = advance(start)

time: 46.8 us -> 46.6 us (level)
  no operation moved by 1% of the time
where the time goes in v7:
time: 46.6 us; the launch traced here: 46.4 us
  blocking collectives  40.5 us (87%)
  Pallas kernels  5.03 us (11%)
  between operations  0.66 us (1%)
    all_to_all x3, blocking collectives, exchange(): return lax.all_to_all(chunks, AXIS, 0, 0, axis_index_groups=groups)  40.5 us
    pallas_call x1, Pallas kernels, local_sums(): pl.pallas_call(gram_kernel, out_shape=pltpu.VMEM((lines, LANES), jnp.floa...  2.83 us
    pallas_call x1, Pallas kernels, solve_and_apply(): pl.pallas_call(lambda *refs: solve_kernel(rows_all, *refs), out_shape=(ja...  2.2 us

profile of v7, /device:TPU:1, one launch (start us, length us, event | category | flops | bytes accessed | tf_op | source)
XLA Modules:
  0.0 46.4 jit_solution(1471669343085113177)
XLA Ops:
  0.6 0.0 copy-start
  0.6 2.8 %gram.1 = f32[160,128]{1,0:T(8,128)S(1)} custom-call(f32[128,32,128]{2,1,0:T(8,128)} %bitcast.26, f32[32,128]{1,0:T(8,128)} %bitcast.27), custom_call_target="tpu_custom_call" | custom-call | tf_op jit(solution)/shard_map/gram/pallas_call | solution.py:205
  3.5 15.2 %all_to_all.15 = f32[32,1,640]{2,1,0:T(1,128)S(1)} all-to-all(f32[32,1,640]{2,1,0:T(1,128)S(1)} %bitcast.25), channel_id=1, replica_groups={{77,0,1,2,3,4,5,6,7,8,9,10,11,12,13,14,15,64,65,66,67,68,69,70,71,72,73..., dimensions={0} | all-to-all | bytes 163840 | tf_op jit(solution)/shard_map/all_to_all | solution.py:239
  18.7 0.1 reduce_sum.18
  18.8 14.9 %all_to_all.16 = f32[16,1,640]{2,1,0:T(1,128)S(1)} all-to-all(f32[16,1,640]{2,1,0:T(1,128)S(1)} %broadcast_in_dim.6), channel_id=1, replica_groups={{288,0,16,32,48,128,144,160,176,256,272,304,384,400,416,432},{289,1,17,..., dimensions={0} | all-to-all | bytes 81920 | tf_op jit(solution)/shard_map/all_to_all | solution.py:239
  33.8 10.4 %all_to_all.17 = f32[32,1,640]{2,1,0:T(1,128)S(1)} all-to-all(f32[32,1,640]{2,1,0:T(1,128)S(1)} %broadcast_in_dim.7), channel_id=1, replica_groups={{77,0,1,2,3,4,5,6,7,8,9,10,11,12,13,14,15,64,65,66,67,68,69,70,71,72,73..., dimensions={0} | all-to-all | bytes 163840 | tf_op jit(solution)/shard_map/all_to_all | solution.py:239
  44.2 0.0 copy-done
  44.2 2.2 %solve.1 = (f32[32,128]{1,0:T(8,128)}, f32[1,128]{1,0:T(1,128)}) custom-call(f32[160,128]{1,0:T(8,128)S(1)} %bitcast.24, f32[128,32,128]{2,1,0:T(8,128)S(1)} %bitcast.23), custom_call_target="tpu_custom_call" | custom-call | tf_op jit(solution)/shard_map/solve/pallas_call | solution.py:223
  (3 shorter events, 0.1 us)
Async XLA Ops:
  0.6 43.6 %copy-start = (f32[128,2,2048]{2,1,0:T(2,128)S(1)}, f32[128,2,2048]{2,1,0:T(2,128)}, u32[]{:S(2)}) copy-start(f32[128,2,2048]{2,1,0:T(2,128)} %param.4) | copy-start | bytes 6291460

commit v8 on v7

--- a/solution.py
+++ b/solution.py
@@ -12,9 +12,9 @@
 TOLERANCE = 1e-06
 STEPS_PER_TEST = 4
 TESTS_MAX = 4
-INNER = ('y0', 'z0', 'x1', 'x0', 'c')
-STEPS = [('y2', 'y1', 'z2', 'z1')]
-ROOT = ('y0', 'z0', 'x1', 'c', 'y2', 'z2')
+INNER = ('z0', 'x1', 'x0', 'c')
+STEPS = [('y2', 'y1', 'y0', 'z2', 'z1')]
+ROOT = ('z0', 'x1', 'c', 'y2', 'z2')
 BITS = ("y2", "y1", "y0", "z2", "z1", "z0", "x1", "x0", "c")
 
 
@@ -26,7 +26,7 @@
         bits = [((device ^ root) >> (count - 1 - k)) & 1 for k in range(count)]
         key = tuple(b for b, name in zip(bits, BITS) if name not in names)
         found.setdefault(key, []).append(device)
-    return [[group[0] ^ root] + [d for d in group if d != group[0] ^ root] for group in map(sorted, found.values())]
+    return [[group[0] ^ root] + [d for d in group if d != group[0] ^ root][::-1] for group in map(sorted, found.values())]
 
 
 def rows_of(x):

time: 46.6 us -> 46.7 us (level)
  no operation moved by 1% of the time
where the time goes in v8:
time: 46.7 us; the launch traced here: 46.5 us
  blocking collectives  40.4 us (87%)
  Pallas kernels  5.06 us (11%)
  between operations  0.67 us (1%)
    all_to_all x3, blocking collectives, exchange(): return lax.all_to_all(chunks, AXIS, 0, 0, axis_index_groups=groups)  40.4 us
    pallas_call x1, Pallas kernels, local_sums(): pl.pallas_call(gram_kernel, out_shape=pltpu.VMEM((lines, LANES), jnp.floa...  2.83 us
    pallas_call x1, Pallas kernels, solve_and_apply(): pl.pallas_call(lambda *refs: solve_kernel(rows_all, *refs), out_shape=(ja...  2.23 us

profile of v8, /device:TPU:1, one launch (start us, length us, event | category | flops | bytes accessed | tf_op | source)
XLA Modules:
  0.0 46.5 jit_solution(837522927848379089)
XLA Ops:
  0.6 0.0 copy-start
  0.6 2.8 %gram.1 = f32[144,128]{1,0:T(8,128)S(1)} custom-call(f32[128,32,128]{2,1,0:T(8,128)} %bitcast.26, f32[32,128]{1,0:T(8,128)} %bitcast.27), custom_call_target="tpu_custom_call" | custom-call | tf_op jit(solution)/shard_map/gram/pallas_call | solution.py:205
  3.5 14.3 %all_to_all.15 = f32[16,1,1152]{2,1,0:T(1,128)S(1)} all-to-all(f32[16,1,1152]{2,1,0:T(1,128)S(1)} %bitcast.25), channel_id=1, replica_groups={{13,15,14,12,11,10,9,8,7,6,5,4,3,2,1,0},{29,31,30,28,27,26,25,24,23,22,..., dimensions={0} | all-to-all | bytes 147456 | tf_op jit(solution)/shard_map/all_to_all | solution.py:239
  17.8 0.1 reduce_sum.18
  17.9 0.1 broadcast_in_dim.6
  17.9 17.2 %all_to_all.16 = f32[32,1,1152]{2,1,0:T(1,128)S(1)} all-to-all(f32[32,1,1152]{2,1,0:T(1,128)S(1)} %broadcast_in_dim.6), channel_id=1, replica_groups={{288,496,480,464,448,432,416,400,384,368,352,336,320,304,272,256,240,22..., dimensions={0} | all-to-all | bytes 294912 | tf_op jit(solution)/shard_map/all_to_all | solution.py:239
  35.2 0.1 reduce_sum.19
  35.3 8.9 %all_to_all.17 = f32[16,1,1152]{2,1,0:T(1,128)S(1)} all-to-all(f32[16,1,1152]{2,1,0:T(1,128)S(1)} %broadcast_in_dim.7), channel_id=1, replica_groups={{13,15,14,12,11,10,9,8,7,6,5,4,3,2,1,0},{29,31,30,28,27,26,25,24,23,22,..., dimensions={0} | all-to-all | bytes 147456 | tf_op jit(solution)/shard_map/all_to_all | solution.py:239
  44.2 0.0 copy-done
  44.2 2.2 %solve.1 = (f32[32,128]{1,0:T(8,128)}, f32[1,128]{1,0:T(1,128)}) custom-call(f32[144,128]{1,0:T(8,128)S(1)} %bitcast.24, f32[128,32,128]{2,1,0:T(8,128)S(1)} %bitcast.23), custom_call_target="tpu_custom_call" | custom-call | tf_op jit(solution)/shard_map/solve/pallas_call | solution.py:223
  (1 shorter events, 0.0 us)
Async XLA Ops:
  0.6 43.6 %copy-start = (f32[128,2,2048]{2,1,0:T(2,128)S(1)}, f32[128,2,2048]{2,1,0:T(2,128)}, u32[]{:S(2)}) copy-start(f32[128,2,2048]{2,1,0:T(2,128)} %param.4) | copy-start | bytes 6291460
